TPU v7x, 1024 devices: a whole 8x8x8 slice. The times are simulated.
1024 devices in a mesh: seq: 32 (over y, x_hi), dp: 32 (over z, x_lo, core).
Axes of the slice: x: 8 (x_hi: 4, x_lo: 2; x = x_hi * 2 + x_lo), y: 8, z: 8, core: 2. Of those that a mesh axis runs over, the one named last changes fastest.
Arguments:
- queries: bfloat16 [262144, 1024], P(('dp', 'seq')), parts along dimension 0, may hold values from -6 to 6
- keys: bfloat16 [262144, 256], P(('dp', 'seq')), parts along dimension 0, may hold values from -6 to 6
- values: bfloat16 [262144, 256], P(('dp', 'seq')), parts along dimension 0, may hold values from -6 to 6
- out_grad: bfloat16 [262144, 1024], P(('dp', 'seq')), parts along dimension 0, may hold values from -6 to 6
- rand_blocks: int32 [4096, 3], P('dp'), parts along dimension 0, may hold values from 0 to 127, as said below
- global_blocks: int32 [64], P('dp'), parts along dimension 0, may hold values from 0 to 127, as said below
Outputs:
- out: bfloat16 [262144, 1024], P(('dp', 'seq')), parts along dimension 0
- query_grad: bfloat16 [262144, 1024], P(('dp', 'seq')), parts along dimension 0
- key_grad: bfloat16 [262144, 256], P(('dp', 'seq')), parts along dimension 0
- value_grad: bfloat16 [262144, 256], P(('dp', 'seq')), parts along dimension 0
There are 32 independent parts, one for each index of `dp`. A program takes and returns all parts, laid end to end along the dimension named above; each array names one. Nothing has to cross between parts.
Inputs may be any that keep to these rules, and one draw needn't show every extreme that they name: `rand_blocks`: block j lies on index j // 4 of seq. For each index r of seq, the 12 entries of rows r * 4 to (r + 1) * 4 - 1 together with the 2 global blocks name blocks of no index more than 1 times, and blocks of some index exactly 1 times. `global_blocks`: the global blocks lie on different indices of seq.
All inputs are finite; a program needn't handle non-finite values.
Results may differ from a plain program's by a relative error of at most 0.011.
Values may be sent and summed in bfloat16 or wider, within the bound.
A program may use at most 32 MiB of HBM per device.

v0:
```python
import jax
import jax.numpy as jnp
from jax import lax
from jax.sharding import PartitionSpec as P

KVH = 2
HD = 128
BLOCK = 64
GLOB = 2
RAND = 3
GROUP = 4


def with_halo(array, sides, width):
    for axis, dim in sides:
        count, length = (lax.axis_size(axis), array.shape[dim])
        up = [(i, (i + 1) % count) for i in range(count)]
        down = [(j, i) for i, j in up]
        last = lax.slice_in_dim(array, length - width, length, axis=dim)
        initial = lax.slice_in_dim(array, 0, width, axis=dim)
        before = lax.ppermute(last, axis, up)
        after = lax.ppermute(initial, axis, down)
        array = jnp.concatenate([before, array, after], axis=dim)
    return array


def attend(inputs):
    query_block, key_set, grad_block = inputs
    rows = query_block.shape[0]
    scale = HD ** (-0.5)
    heads_q = query_block.reshape(rows, KVH, GROUP, HD)
    grads_q = grad_block.reshape(rows, KVH, GROUP, HD)
    keys_all = key_set[:, :, 0].reshape(-1, KVH, HD)
    values_all = key_set[:, :, 1].reshape(-1, KVH, HD)
    scores = (
        jnp.einsum("qgjd,kgd->gjqk", heads_q, keys_all, preferred_element_type=jnp.float32) * scale
    )
    peak = jnp.max(scores, axis=-1, keepdims=True)
    expos = jnp.exp(scores - peak)
    probs = expos / jnp.sum(expos, axis=-1, keepdims=True)
    probs_b = probs.astype(jnp.bfloat16)
    attended = jnp.einsum("gjqk,kgd->qgjd", probs_b, values_all, preferred_element_type=jnp.float32)
    delta = jnp.transpose(jnp.sum(grads_q.astype(jnp.float32) * attended, axis=-1), (1, 2, 0))
    dprobs = jnp.einsum("qgjd,kgd->gjqk", grads_q, values_all, preferred_element_type=jnp.float32)
    dscores = (probs * (dprobs - delta[..., None]) * scale).astype(jnp.bfloat16)
    qgrad = jnp.einsum("gjqk,kgd->qgjd", dscores, keys_all, preferred_element_type=jnp.float32)
    key_part = jnp.einsum("gjqk,qgjd->kgd", dscores, heads_q, preferred_element_type=jnp.float32)
    value_part = jnp.einsum("gjqk,qgjd->kgd", probs_b, grads_q, preferred_element_type=jnp.float32)
    terms = jnp.stack([key_part.reshape(-1, KVH * HD), value_part.reshape(-1, KVH * HD)], axis=1)
    terms = terms.reshape(key_set.shape[0], rows, 2, KVH * HD)
    return (
        attended.reshape(rows, -1).astype(jnp.bfloat16),
        qgrad.reshape(rows, -1).astype(jnp.bfloat16),
        terms,
    )


def local(queries, keys, values, out_grad, rand_blocks, global_blocks):
    cycle_size = lax.axis_size("seq")
    myself = lax.axis_index("seq")
    tok_rows = queries.shape[0]
    blocks_here = tok_rows // BLOCK
    feature = keys.shape[1]
    capacity = (RAND * blocks_here + GLOB + cycle_size - 1) // cycle_size
    rand_total = RAND * blocks_here
    slot_total = cycle_size * capacity
    key_value = jnp.stack([keys, values], axis=1)
    widened = with_halo(key_value, (("seq", 0),), BLOCK)
    widened = widened.reshape(blocks_here + 2, BLOCK, 2, feature)
    window = jnp.stack(
        [widened[0:blocks_here], widened[1 : blocks_here + 1], widened[2 : blocks_here + 2]], axis=1
    )
    own_blocks = key_value.reshape(blocks_here, BLOCK, 2, feature)
    listed = jnp.concatenate(
        [
            rand_blocks.reshape(cycle_size, rand_total),
            jnp.broadcast_to(global_blocks[None, :], (cycle_size, GLOB)),
        ],
        axis=1,
    )
    entries = listed.shape[1]
    owners = listed // blocks_here
    local_slot = listed % blocks_here
    earlier = jnp.arange(entries)[None, :] < jnp.arange(entries)[:, None]
    same_owner = owners[:, :, None] == owners[:, None, :]
    ranking = jnp.sum(same_owner & earlier[None], axis=2)
    owners_mine = lax.dynamic_index_in_dim(owners, myself, 0, keepdims=False)
    ranking_mine = lax.dynamic_index_in_dim(ranking, myself, 0, keepdims=False)
    row_mine = owners_mine * capacity + ranking_mine
    slot_ids = jnp.arange(slot_total)
    requester = slot_ids // capacity
    position = slot_ids % capacity
    matches = (owners[requester] == myself) & (ranking[requester] == position[:, None])
    filled = jnp.any(matches, axis=1)
    source = jnp.sum(jnp.where(matches, local_slot[requester], 0), axis=1)
    outgoing = jnp.where(
        filled[:, None, None, None],
        jnp.take(own_blocks, source, axis=0),
        jnp.zeros((), jnp.bfloat16),
    )
    incoming = lax.all_to_all(outgoing, "seq", split_axis=0, concat_axis=0, tiled=True)
    far_pairs = jnp.take(incoming, row_mine, axis=0)
    global_pairs = far_pairs[rand_total : rand_total + GLOB]
    random_pairs = far_pairs[:rand_total].reshape(blocks_here, RAND, BLOCK, 2, feature)
    key_sets = jnp.concatenate(
        [
            window,
            jnp.broadcast_to(global_pairs[None], (blocks_here, GLOB, BLOCK, 2, feature)),
            random_pairs,
        ],
        axis=1,
    )
    query_blocks = queries.reshape(blocks_here, BLOCK, -1)
    grad_blocks = out_grad.reshape(blocks_here, BLOCK, -1)
    out_blocks, qgrad_blocks, key_terms = lax.map(attend, (query_blocks, key_sets, grad_blocks))
    window_terms = key_terms[:, :3]
    extended = jnp.pad(window_terms[:, 0], ((0, 2), (0, 0), (0, 0), (0, 0)))
    extended = extended + jnp.pad(window_terms[:, 1], ((1, 1), (0, 0), (0, 0), (0, 0)))
    extended = extended + jnp.pad(window_terms[:, 2], ((2, 0), (0, 0), (0, 0), (0, 0)))
    rim_terms = jnp.concatenate([extended[0], extended[blocks_here + 1]], axis=0)
    returned_rims = with_halo(rim_terms, (("seq", 0),), BLOCK)
    gathered = extended[1 : blocks_here + 1]
    gathered = gathered.at[0].add(returned_rims[:BLOCK])
    gathered = gathered.at[blocks_here - 1].add(returned_rims[3 * BLOCK :])
    rand_grad = key_terms[:, 3 + GLOB :].reshape(rand_total, BLOCK, 2, feature).astype(jnp.bfloat16)
    glob_grad = jnp.sum(key_terms[:, 3 : 3 + GLOB], axis=0).astype(jnp.bfloat16)
    far_grad = jnp.concatenate([rand_grad, glob_grad], axis=0)
    placing = (row_mine[None, :] == slot_ids[:, None]).astype(jnp.bfloat16)
    returning = jnp.einsum(
        "sf,fbcx->sbcx", placing, far_grad, preferred_element_type=jnp.float32
    ).astype(jnp.bfloat16)
    received = lax.all_to_all(returning, "seq", split_axis=0, concat_axis=0, tiled=True)
    landing = (filled[:, None] & (source[:, None] == jnp.arange(blocks_here)[None, :])).astype(
        jnp.bfloat16
    )
    gathered = gathered + jnp.einsum(
        "sq,sbcx->qbcx", landing, received, preferred_element_type=jnp.float32
    )
    out = out_blocks.reshape(tok_rows, -1)
    query_grad = qgrad_blocks.reshape(tok_rows, -1)
    key_grad = gathered[:, :, 0].reshape(tok_rows, feature).astype(jnp.bfloat16)
    value_grad = gathered[:, :, 1].reshape(tok_rows, feature).astype(jnp.bfloat16)
    return (out, query_grad, key_grad, value_grad)


def solution(mesh):
    in_specs = (
        P(("dp", "seq"), None),
        P(("dp", "seq"), None),
        P(("dp", "seq"), None),
        P(("dp", "seq"), None),
        P("dp", None),
        P("dp"),
    )
    out_specs = (
        P(("dp", "seq"), None),
        P(("dp", "seq"), None),
        P(("dp", "seq"), None),
        P(("dp", "seq"), None),
    )
    return jax.shard_map(local, mesh=mesh, in_specs=in_specs, out_specs=out_specs, check_vma=False)
```

profile of v0, /device:TPU:698, one launch (start us, length us, event | category | flops | bytes accessed | tf_op | source)
XLA Modules:
  0.0 228.0 jit_solution(807028845875461875)
XLA Ops:
  0.7 0.8 copy.115
  1.5 0.7 pad.26.clone
  4.6 1.0 pad_maximum_fusion.5
  5.6 0.7 gather_fusion.3
  6.3 1.7 select_select_fusion
  8.0 12.5 %all-to-all-start = ((bf16[32,64,2,256]{3,1,2,0:T(8,128)(2,1)}), bf16[32,64,2,256]{3,1,2,0:T(8,128)(2,1)S(1)}, u32[]{:S(2)}, u32[]{:S(2)}) async-start(bf16[32,64,2,256]{3,1,2,0:T(8,128)(2,1)} %select_select_fusion), calls=%async_computation | async-start | bytes 4194304 | tf_op jit(solution)/shard_map/all_to_all | solution.py:101
  20.5 2.5 %collective-permute-start.1 = (bf16[64,2,256]{2,0,1:T(8,128)(2,1)S(1)}, bf16[64,2,256]{2,0,1:T(8,128)(2,1)S(1)}, u32[]{:S(2)}, u32[]{:S(2)}) collective-permute-start(bf16[64,2,256]{2,0,1:T(8,128)(2,1)S(1)} %get-tuple-element.106), channel_id=1, source_target_pairs={{32,0},{64,32},{96,64},{128,96},{160,128},{192,160},{224,192},{256... | collective-permute-start | bytes 196616 | tf_op jit(solution)/shard_map/ppermute | solution.py:22
  23.0 4.3 %collective-permute-start = (bf16[64,2,256]{2,0,1:T(8,128)(2,1)S(1)}, bf16[64,2,256]{2,0,1:T(8,128)(2,1)S(1)}, u32[]{:S(2)}, u32[]{:S(2)}) collective-permute-start(bf16[64,2,256]{2,0,1:T(8,128)(2,1)S(1)} %get-tuple-element.107), channel_id=1, source_target_pairs={{0,32},{32,64},{64,96},{96,128},{128,160},{160,192},{192,224},{224... | collective-permute-start | bytes 196616 | tf_op jit(solution)/shard_map/ppermute | solution.py:21
  27.4 52.6 %collective-permute-done.1 = bf16[64,2,256]{2,0,1:T(8,128)(2,1)S(1)} collective-permute-done((bf16[64,2,256]{2,0,1:T(8,128)(2,1)S(1)}, bf16[64,2,256]{2,0,1:T(8,128)(2,1)S(1)}, u32[]{:S(2)}, u32[]{:S(2)}) %collective-permute-start.1) | collective-permute-done | bytes 65568 | tf_op jit(solution)/shard_map/ppermute | solution.py:22
  80.0 0.7 copy_dynamic-update-slice_fusion.3
  80.7 0.7 copy_dynamic-update-slice_fusion.2
  81.5 0.7 copy_dynamic-update-slice_fusion.1
  83.0 0.9 broadcast_dynamic-update-slice_fusion
  83.9 1.0 copy_dynamic-update-slice_fusion
  84.9 50.6 %while.16 = (s32[]{:T(128)}, bf16[4,64,1024]{2,1,0:T(8,128)(2,1)S(1)}, bf16[4,64,1024]{2,1,0:T(8,128)(2,1)}, f32[4,8,64,2,256]{4,2,1,3,0:T(8,128)}, bf16[4,8,64,...) while((s32[]{:T(128)}, ...), condition=%wide.region_7.8_spmd, body=%wide.region_3.7_spmd.sunk | while | flops 541657088 | bytes 19542128 | solution.py:115
  84.9 0.9 constant_dynamic-slice_fusion.6
  85.9 0.9 constant_dynamic-slice_fusion.7
  86.9 1.1 dynamic-slice_bitcast_fusion.2
  88.2 1.4 fusion.122
  89.6 1.2 multiply_reduce_fusion.2
  90.8 1.6 fusion.123
  93.0 1.1 convolution_bitcast_fusion.6
  95.8 0.7 constant_dynamic-update-slice_fusion.3
  96.5 1.1 maximum_dynamic-update-slice_fusion.2
  97.5 0.9 constant_dynamic-slice_fusion.6
  98.5 0.9 constant_dynamic-slice_fusion.7
  99.5 1.1 dynamic-slice_bitcast_fusion.2
  100.8 1.4 fusion.122
  102.2 1.2 multiply_reduce_fusion.2
  103.5 1.6 fusion.123
  105.6 1.1 convolution_bitcast_fusion.6
  108.4 0.7 constant_dynamic-update-slice_fusion.3
  109.1 1.1 maximum_dynamic-update-slice_fusion.2
  110.2 0.9 constant_dynamic-slice_fusion.6
  111.2 0.9 constant_dynamic-slice_fusion.7
  112.2 1.1 dynamic-slice_bitcast_fusion.2
  113.5 1.4 fusion.122
  114.9 1.2 multiply_reduce_fusion.2
  116.1 1.6 fusion.123
  118.3 1.1 convolution_bitcast_fusion.6
  121.1 0.7 constant_dynamic-update-slice_fusion.3
  121.8 1.1 maximum_dynamic-update-slice_fusion.2
  122.8 0.9 constant_dynamic-slice_fusion.6
  123.8 0.9 constant_dynamic-slice_fusion.7
  124.8 1.1 dynamic-slice_bitcast_fusion.2
  126.1 1.4 fusion.122
  127.5 1.2 multiply_reduce_fusion.2
  128.8 1.6 fusion.123
  130.9 1.1 convolution_bitcast_fusion.6
  133.7 0.7 constant_dynamic-update-slice_fusion.3
  134.4 1.0 maximum_dynamic-update-slice_fusion.2
  135.5 1.5 slice_reduce_fusion
  137.0 2.5 %copy.130 = bf16[4,8,64,2,256]{4,2,3,1,0:T(8,128)(2,1)S(1)} copy(f32[4,8,64,2,256]{4,2,1,3,0:T(8,128)} %get-tuple-element.69) | data formatting | bytes 6291456 | tf_op jit(solution)/shard_map/while | solution.py:115
  140.1 0.8 convolution_convert_fusion.1
  141.0 3.5 %copy.133 = bf16[32,64,2,256]{3,2,1,0:T(2,128)(2,1)} copy(bf16[32,64,2,256]{3,0,2,1:T(8,128)(2,1)S(1)} %convolution_convert_fusion.1) | data formatting | bytes 4194304 | tf_op jit(solution)/shard_map/convert_element_type | solution.py:131
  144.4 10.1 %all-to-all-start.1 = ((bf16[32,64,2,256]{3,2,1,0:T(2,128)(2,1)}), bf16[32,64,2,256]{3,2,1,0:T(2,128)(2,1)S(1)}, u32[]{:S(2)}, u32[]{:S(2)}) async-start(bf16[32,64,2,256]{3,2,1,0:T(2,128)(2,1)} %copy.133), calls=%async_computation.1 | async-start | bytes 4194304 | tf_op jit(solution)/shard_map/all_to_all | solution.py:132
  154.5 5.5 %copy.125 = f32[4,8,64,2,256]{4,3,2,0,1:T(2,128)S(1)} copy(f32[4,8,64,2,256]{4,2,1,3,0:T(8,128)} %get-tuple-element.69) | data formatting | bytes 8388608 | tf_op jit(solution)/shard_map/while | solution.py:115
  160.6 2.5 %collective-permute-start.3 = (f32[64,2,256]{2,1,0:T(2,128)S(1)}, f32[64,2,256]{2,1,0:T(2,128)S(1)}, u32[]{:S(2)}, u32[]{:S(2)}) collective-permute-start(f32[64,2,256]{2,1,0:T(2,128)S(1)} %get-tuple-element.100), channel_id=1, source_target_pairs={{32,0},{64,32},{96,64},{128,96},{160,128},{192,160},{224,192},{256... | collective-permute-start | bytes 393224 | tf_op jit(solution)/shard_map/ppermute | solution.py:22
  163.1 4.3 %collective-permute-start.2 = (f32[64,2,256]{2,1,0:T(2,128)S(1)}, f32[64,2,256]{2,1,0:T(2,128)S(1)}, u32[]{:S(2)}, u32[]{:S(2)}) collective-permute-start(f32[64,2,256]{2,1,0:T(2,128)S(1)} %get-tuple-element.101), channel_id=1, source_target_pairs={{0,32},{32,64},{64,96},{96,128},{128,160},{160,192},{192,224},{224... | collective-permute-start | bytes 393224 | tf_op jit(solution)/shard_map/ppermute | solution.py:21
  168.0 36.5 %collective-permute-done.2 = f32[64,2,256]{2,1,0:T(2,128)S(1)} collective-permute-done((f32[64,2,256]{2,1,0:T(2,128)S(1)}, f32[64,2,256]{2,1,0:T(2,128)S(1)}, u32[]{:S(2)}, u32[]{:S(2)}) %collective-permute-start.2) | collective-permute-done | bytes 131104 | tf_op jit(solution)/shard_map/ppermute | solution.py:21
  204.9 18.4 %collective-permute-done.3 = f32[64,2,256]{2,1,0:T(2,128)S(1)} collective-permute-done((f32[64,2,256]{2,1,0:T(2,128)S(1)}, f32[64,2,256]{2,1,0:T(2,128)S(1)}, u32[]{:S(2)}, u32[]{:S(2)}) %collective-permute-start.3) | collective-permute-done | bytes 131104 | tf_op jit(solution)/shard_map/ppermute | solution.py:22
  223.5 1.8 scatter-add.9
  225.3 1.3 fusion.51
  226.7 0.7 copy.136
  (111 shorter events, 16.6 us)
Async XLA Ops:
  7.9 12.5 %copy-start = (bf16[256,256]{1,0:T(8,128)(2,1)S(1)}, bf16[256,256]{1,0:T(8,128)(2,1)}, u32[]{:S(2)}) copy-start(bf16[256,256]{1,0:T(8,128)(2,1)} %param.14) | copy-start | bytes 393220
  8.0 12.6 %copy-start.1 = (bf16[256,256]{1,0:T(8,128)(2,1)S(1)}, bf16[256,256]{1,0:T(8,128)(2,1)}, u32[]{:S(2)}) copy-start(bf16[256,256]{1,0:T(8,128)(2,1)} %param.13) | copy-start | bytes 393220
  8.0 74.2 %all-to-all-start = ((bf16[32,64,2,256]{3,1,2,0:T(8,128)(2,1)}), bf16[32,64,2,256]{3,1,2,0:T(8,128)(2,1)S(1)}, u32[]{:S(2)}, u32[]{:S(2)}) async-start(bf16[32,64,2,256]{3,1,2,0:T(8,128)(2,1)} %select_select_fusion), calls=%async_computation | async-start | bytes 4194304 | tf_op jit(solution)/shard_map/all_to_all | solution.py:101
  20.5 59.4 %collective-permute-start.1 = (bf16[64,2,256]{2,0,1:T(8,128)(2,1)S(1)}, bf16[64,2,256]{2,0,1:T(8,128)(2,1)S(1)}, u32[]{:S(2)}, u32[]{:S(2)}) collective-permute-start(bf16[64,2,256]{2,0,1:T(8,128)(2,1)S(1)} %get-tuple-element.106), channel_id=1, source_target_pairs={{32,0},{64,32},{96,64},{128,96},{160,128},{192,160},{224,192},{256... | collective-permute-start | bytes 196616 | tf_op jit(solution)/shard_map/ppermute | solution.py:22
  23.0 57.0 %collective-permute-start = (bf16[64,2,256]{2,0,1:T(8,128)(2,1)S(1)}, bf16[64,2,256]{2,0,1:T(8,128)(2,1)S(1)}, u32[]{:S(2)}, u32[]{:S(2)}) collective-permute-start(bf16[64,2,256]{2,0,1:T(8,128)(2,1)S(1)} %get-tuple-element.107), channel_id=1, source_target_pairs={{0,32},{32,64},{64,96},{96,128},{128,160},{160,192},{192,224},{224... | collective-permute-start | bytes 196616 | tf_op jit(solution)/shard_map/ppermute | solution.py:21
  82.9 1.9 copy-start.2
  135.5 4.0 %copy-start.3 = (bf16[4,64,1024]{2,1,0:T(8,128)(2,1)}, bf16[4,64,1024]{2,1,0:T(8,128)(2,1)S(1)}, u32[]{:S(2)}) copy-start(bf16[4,64,1024]{2,1,0:T(8,128)(2,1)S(1)} %get-tuple-element.67) | copy-start | bytes 1572868
  144.4 80.8 %all-to-all-start.1 = ((bf16[32,64,2,256]{3,2,1,0:T(2,128)(2,1)}), bf16[32,64,2,256]{3,2,1,0:T(2,128)(2,1)S(1)}, u32[]{:S(2)}, u32[]{:S(2)}) async-start(bf16[32,64,2,256]{3,2,1,0:T(2,128)(2,1)} %copy.133), calls=%async_computation.1 | async-start | bytes 4194304 | tf_op jit(solution)/shard_map/all_to_all | solution.py:132
  160.6 62.7 %collective-permute-start.3 = (f32[64,2,256]{2,1,0:T(2,128)S(1)}, f32[64,2,256]{2,1,0:T(2,128)S(1)}, u32[]{:S(2)}, u32[]{:S(2)}) collective-permute-start(f32[64,2,256]{2,1,0:T(2,128)S(1)} %get-tuple-element.100), channel_id=1, source_target_pairs={{32,0},{64,32},{96,64},{128,96},{160,128},{192,160},{224,192},{256... | collective-permute-start | bytes 393224 | tf_op jit(solution)/shard_map/ppermute | solution.py:22
  163.1 41.4 %collective-permute-start.2 = (f32[64,2,256]{2,1,0:T(2,128)S(1)}, f32[64,2,256]{2,1,0:T(2,128)S(1)}, u32[]{:S(2)}, u32[]{:S(2)}) collective-permute-start(f32[64,2,256]{2,1,0:T(2,128)S(1)} %get-tuple-element.101), channel_id=1, source_target_pairs={{0,32},{32,64},{64,96},{96,128},{128,160},{160,192},{192,224},{224... | collective-permute-start | bytes 393224 | tf_op jit(solution)/shard_map/ppermute | solution.py:21
where the time goes:
time: 229 us; the launch traced here: 228 us
  waiting for transfers between devices  107 us (47%)
  local copies, waits for them, and re-layouts  46.8 us (20%)
  starting transfers between devices  36.1 us (16%)
  matrix products  25.6 us (11%)
  other arithmetic  10.5 us (5%)
    ppermute x2, waiting for transfers between devices, with_halo(): after = lax.ppermute(initial, axis, down)  71 us
    ppermute x2, waiting for transfers between devices, with_halo(): before = lax.ppermute(last, axis, up)  36.5 us
    all_to_all x1, starting transfers between devices, local(): lax.all_to_all(outgoing, 'seq', split_axis=0, concat_axis=0, tiled=True)  12.5 us
    all_to_all x1, starting transfers between devices, local(): lax.all_to_all(returning, 'seq', split_axis=0, concat_axis=0, tiled=True)  10.1 us
    ppermute x2, starting transfers between devices, with_halo(): before = lax.ppermute(last, axis, up)  8.54 us
    while x2, local copies, waits for them, and re-layouts, local(): lax.map(attend, (query_blocks, key_sets, grad_blocks))  7.99 us
    dynamic_slice x8, local copies, waits for them, and re-layouts, local(): lax.map(attend, (query_blocks, key_sets, grad_blocks))  7.33 us
    dot_general x4, matrix products, attend(): jnp.einsum('qgjd,kgd->gjqk', grads_q, values_all, preferred_element_type=...  6.22 us
  transfers between devices with their start and end apart: 6, of which 3 were waited for; matrix products, arithmetic and copies ran while one was open for 5% of the time, Pallas kernels for 0%

commit v1 on v0

v1 whole, which is shorter than its diff:
```python
import math

import jax
import jax.numpy as jnp
from jax import lax
from jax.experimental import pallas as pl
from jax.experimental.pallas import tpu as pltpu
from jax.sharding import PartitionSpec as P

KVH = 2
HD = 128
BLOCK = 64
GLOB = 2
RAND = 3
GROUP = 4
QB = 4
NY = 8
NX = 4
FAR = RAND * QB + GLOB
KEYS = (3 + GLOB + RAND) * BLOCK
TOK = QB * BLOCK
SCALE = HD ** (-0.5)
LOG2E = math.log2(math.e)
F32 = jnp.float32
BF16 = jnp.bfloat16


def dot_nt(a, b):
    return lax.dot_general(a, b, (((1,), (1,)), ((), ())), preferred_element_type=F32)


def dot_nn(a, b):
    return lax.dot_general(a, b, (((1,), (0,)), ((), ())), preferred_element_type=F32)


def dot_tn(a, b):
    return lax.dot_general(a, b, (((0,), (0,)), ((), ())), preferred_element_type=F32)


HEAD_BUFFERS = (
    ("xg", (NX * QB, BLOCK, HD), BF16),
    ("yg", (NY * QB, BLOCK, HD), BF16),
    ("sk", (NY * NX, BLOCK, HD), BF16),
    ("rk", (NY * NX, BLOCK, HD), BF16),
    ("sv", (NX * NY, BLOCK, HD), BF16),
    ("rv", (NX * NY, BLOCK, HD), BF16),
    ("fk", (FAR, BLOCK, HD), BF16),
    ("fv", (FAR, BLOCK, HD), BF16),
    ("bsk", (NY * NX, BLOCK, HD), BF16),
    ("brk", (NY * NX, BLOCK, HD), BF16),
    ("bsv", (NX * NY, BLOCK, HD), BF16),
    ("brv", (NX * NY, BLOCK, HD), BF16),
    ("ak", (NX, TOK, HD), BF16),
    ("rak", (NX, TOK, HD), BF16),
    ("av", (NY, TOK, HD), F32),
    ("su", (4, TOK, HD), BF16),
    ("ru", (4, TOK, HD), BF16),
    ("sd", (4, TOK, HD), BF16),
    ("rd", (4, TOK, HD), BF16),
    ("kx", ((QB + 2) * BLOCK, HD), BF16),
    ("vx", ((QB + 2) * BLOCK, HD), BF16),
    ("wk", ((QB + 2) * BLOCK, HD), F32),
    ("wv", ((QB + 2) * BLOCK, HD), F32),
    ("gk", (GLOB * BLOCK, HD), F32),
    ("gv", (GLOB * BLOCK, HD), F32),
    ("rim_out", (2, 2, BLOCK, HD), BF16),
    ("rim_in", (2, 2, BLOCK, HD), BF16),
)
HEAD_COPIES = (
    ("xs", NX - 1), ("up", 4), ("down", 4), ("ks", NY - 1), ("vs", NX - 1),
    ("bks", NY - 1), ("bvs", NX - 1), ("axs", NX - 1), ("bup", 4), ("bdown", 4), ("rim", 4),
)


class Named:
    def __init__(self, names, refs):
        for name, ref in zip(names, refs, strict=True):
            setattr(self, name, ref)


def kernel(rb, gb, q_ref, k_ref, v_ref, g_ref, out_ref, qg_ref, kg_ref, vg_ref, *scratch):
    scratch = list(scratch)

    def take(n):
        got = scratch[:n]
        del scratch[:n]
        return got

    tk, tv, ent, halo, kc, vc = take(6)
    bufs = [Named([b[0] for b in HEAD_BUFFERS], take(len(HEAD_BUFFERS))) for _ in range(KVH)]
    halo_sems = take(2)
    sems = []
    for _ in range(KVH):
        refs = take(2 * len(HEAD_COPIES))
        sems.append(Named([c[0] for c in HEAD_COPIES], [(refs[2 * i], refs[2 * i + 1]) for i in range(len(HEAD_COPIES))]))

    me = lax.axis_index("seq")
    y, x = lax.div(me, NX), lax.rem(me, NX)

    def at(row, col):
        return lax.rem(row, NY) * NX + lax.rem(col, NX)

    col_peers = [at(y + d, x) for d in range(1, NY)]
    row_peers = [at(y, x + d) for d in range(1, NX)]
    up, down = at(y + 1, x), at(y + NY - 1, x)
    after = lax.rem(me + 1, NY * NX)
    before = lax.rem(me + NY * NX - 1, NY * NX)
    barrier = pltpu.get_barrier_semaphore()
    peers = col_peers + row_peers + [after, before]
    for peer in peers:
        pl.semaphore_signal(barrier, inc=1, device_id={"seq": peer}, device_id_type=pl.DeviceIdType.MESH)

    started = []

    def copy(src, dst, pair, i, peer):
        return pltpu.make_async_remote_copy(
            src_ref=src, dst_ref=dst, send_sem=pair[0].at[i], recv_sem=pair[1].at[i],
            device_id={"seq": peer}, device_id_type=pl.DeviceIdType.MESH,
        )

    def send(src, dst, pair, i, peer):
        c = copy(src, dst, pair, i, peer)
        c.start()
        started.append(c)

    def arrive(dst, pair, i):
        copy(dst, dst, pair, i, after).wait_recv()

    for h, b in enumerate(bufs):
        cols = slice(h * HD, (h + 1) * HD)
        b.xg[pl.ds(x * QB, QB)] = k_ref[:, cols].reshape(QB, BLOCK, HD)
        b.yg[pl.ds(y * QB, QB)] = v_ref[:, cols].reshape(QB, BLOCK, HD)
        b.kx[BLOCK : BLOCK + TOK] = k_ref[:, cols]
        b.vx[BLOCK : BLOCK + TOK] = v_ref[:, cols]

    pl.semaphore_wait(barrier, len(peers))

    for h, b in enumerate(bufs):
        cols = slice(h * HD, (h + 1) * HD)
        own = b.yg.at[pl.ds(y * QB, QB)]
        send(own, own, sems[h].up, 0, up)
        send(own, own, sems[h].down, 0, down)
        own = b.xg.at[pl.ds(x * QB, QB)]
        for i, peer in enumerate(row_peers):
            send(own, own, sems[h].xs, i, peer)
    send(k_ref.at[TOK - BLOCK : TOK], halo.at[0, 0], halo_sems, 0, after)
    send(v_ref.at[TOK - BLOCK : TOK], halo.at[0, 1], halo_sems, 1, after)
    send(k_ref.at[0:BLOCK], halo.at[1, 0], halo_sems, 2, before)
    send(v_ref.at[0:BLOCK], halo.at[1, 1], halo_sems, 3, before)

    def listed(device):
        ids = [rb[device * QB + e // RAND, e % RAND] for e in range(RAND * QB)]
        return ids + [gb[e] for e in range(GLOB)]

    def named(ids, owner, pick):
        found = jnp.int32(-1)
        for e, block in enumerate(ids):
            found = jnp.where((block >> 2) == owner, pick(e, block), found)
        return found

    @pl.loop(0, NY)
    def _(row):
        ids = listed(row * NX + x)
        for c in range(NX):
            tk[row * NX + c] = named(ids, y * NX + c, lambda e, block: block & 3)

    @pl.loop(0, NX)
    def _(col):
        ids = listed(y * NX + col)
        for r in range(NY):
            tv[col * NY + r] = named(ids, r * NX + x, lambda e, block: block & 3)

    mine = listed(me)

    @pl.loop(0, NY * NX)
    def _(owner):
        ent[owner] = jnp.maximum(named(mine, owner, lambda e, block: jnp.int32(e)), 0)

    half = TOK // 2
    for s in range(1, 4):
        for h, b in enumerate(bufs):
            lower, upper = lax.rem(y + NY - s, NY) * QB, lax.rem(y + s, NY) * QB
            n = QB if s < 3 else QB // 2
            arrive(b.yg.at[pl.ds(lower, QB)], sems[h].up, s - 1)
            part = b.yg.at[pl.ds(lower, n)]
            send(part, part, sems[h].up, s, up)
            arrive(b.yg.at[pl.ds(upper, QB)], sems[h].down, s - 1)
            part = b.yg.at[pl.ds(upper + QB - n, n)]
            send(part, part, sems[h].down, s, down)

    across = lax.rem(y + 4, NY)
    for h, b in enumerate(bufs):
        for i, d in enumerate(range(1, NX)):
            arrive(b.xg.at[pl.ds(lax.rem(x + NX - d, NX) * QB, QB)], sems[h].xs, i)

        @pl.loop(0, NY)
        def _(row):
            for c in range(NX):
                b.sk[row * NX + c] = b.xg[c * QB + jnp.maximum(tk[row * NX + c], 0)]

        for i, d in enumerate(range(1, NY)):
            row = lax.rem(y + d, NY)
            send(b.sk.at[pl.ds(row * NX, NX)], b.rk.at[pl.ds(y * NX, NX)], sems[h].ks, i, col_peers[i])
        b.rk[pl.ds(y * NX, NX)] = b.sk[pl.ds(y * NX, NX)]
        arrive(b.yg.at[pl.ds(across * QB, QB // 2)], sems[h].up, 3)
        arrive(b.yg.at[pl.ds(across * QB + QB // 2, QB // 2)], sems[h].down, 3)

        @pl.loop(0, NX)
        def _(col):
            for r in range(NY):
                b.sv[col * NY + r] = b.yg[r * QB + jnp.maximum(tv[col * NY + r], 0)]

        for i, d in enumerate(range(1, NX)):
            col = lax.rem(x + d, NX)
            send(b.sv.at[pl.ds(col * NY, NY)], b.rv.at[pl.ds(x * NY, NY)], sems[h].vs, i, row_peers[i])
        b.rv[pl.ds(x * NY, NY)] = b.sv[pl.ds(x * NY, NY)]

    for i in range(4):
        arrive(halo.at[i // 2, i % 2], halo_sems, i)
    for h, b in enumerate(bufs):
        cols = slice(h * HD, (h + 1) * HD)
        b.kx[0:BLOCK] = halo[0, 0, :, cols]
        b.vx[0:BLOCK] = halo[0, 1, :, cols]
        b.kx[BLOCK + TOK :] = halo[1, 0, :, cols]
        b.vx[BLOCK + TOK :] = halo[1, 1, :, cols]

    def compute(h):
        b = bufs[h]
        for ref in (b.wk, b.wv, b.gk, b.gv):
            ref[...] = jnp.zeros_like(ref)
        window, globe = 3 * BLOCK, GLOB * BLOCK
        for i in range(GLOB):
            owner = gb[i] >> 2
            kc[window + i * BLOCK : window + (i + 1) * BLOCK] = b.rk[owner]
            vc[window + i * BLOCK : window + (i + 1) * BLOCK] = b.rv[(owner & 3) * NY + (owner >> 2)]

        @pl.loop(0, QB)
        def _(j):
            rows = pl.ds(pl.multiple_of(j * BLOCK, BLOCK), BLOCK)
            span = pl.ds(pl.multiple_of(j * BLOCK, BLOCK), window)
            kc[0:window] = b.kx[span]
            vc[0:window] = b.vx[span]
            for i in range(RAND):
                owner = rb[me * QB + j, i] >> 2
                to = slice(window + globe + i * BLOCK, window + globe + (i + 1) * BLOCK)
                kc[to] = b.rk[owner]
                vc[to] = b.rv[(owner & 3) * NY + (owner >> 2)]
            base = h * GROUP * HD
            q = jnp.concatenate([q_ref[rows, base + i * HD : base + (i + 1) * HD] for i in range(GROUP)], axis=0)
            g = jnp.concatenate([g_ref[rows, base + i * HD : base + (i + 1) * HD] for i in range(GROUP)], axis=0)
            k, v = kc[...], vc[...]
            scores = dot_nt(q, k)
            peak = jnp.max(scores, axis=1, keepdims=True)
            expos = jnp.exp2((scores - peak) * (SCALE * LOG2E))
            probs = expos * (1.0 / jnp.sum(expos, axis=1, keepdims=True))
            probs_b = probs.astype(BF16)
            attended = dot_nn(probs_b, v)
            delta = jnp.sum(g.astype(F32) * attended, axis=1, keepdims=True)
            dprobs = dot_nt(g, v)
            dscores = (probs * (dprobs - delta)).astype(BF16)
            qgrad = dot_nn(dscores, k) * SCALE
            for i in range(GROUP):
                part = slice(i * BLOCK, (i + 1) * BLOCK)
                out_ref[rows, base + i * HD : base + (i + 1) * HD] = attended[part].astype(BF16)
                qg_ref[rows, base + i * HD : base + (i + 1) * HD] = qgrad[part].astype(BF16)
            key_part = dot_tn(dscores, q) * SCALE
            b.wk[span] += key_part[:window]
            b.gk[...] += key_part[window : window + globe]
            b.fk[pl.ds(j * RAND, RAND)] = key_part[window + globe :].astype(BF16).reshape(RAND, BLOCK, HD)
            value_part = dot_tn(probs_b, g)
            b.wv[span] += value_part[:window]
            b.gv[...] += value_part[window : window + globe]
            b.fv[pl.ds(j * RAND, RAND)] = value_part[window + globe :].astype(BF16).reshape(RAND, BLOCK, HD)

        b.fk[RAND * QB :] = b.gk[...].astype(BF16).reshape(GLOB, BLOCK, HD)
        b.fv[RAND * QB :] = b.gv[...].astype(BF16).reshape(GLOB, BLOCK, HD)

    def send_back(h):
        b = bufs[h]

        @pl.loop(0, NY * NX)
        def _(owner):
            b.bsk[owner] = b.fk[ent[owner]]

        for i, d in enumerate(range(1, NY)):
            row = lax.rem(y + d, NY)
            send(b.bsk.at[pl.ds(row * NX, NX)], b.brk.at[pl.ds(y * NX, NX)], sems[h].bks, i, col_peers[i])

        @pl.loop(0, NX)
        def _(col):
            for r in range(NY):
                b.bsv[col * NY + r] = b.fv[ent[r * NX + col]]

        for i, d in enumerate(range(1, NX)):
            col = lax.rem(x + d, NX)
            send(b.bsv.at[pl.ds(col * NY, NY)], b.brv.at[pl.ds(x * NY, NY)], sems[h].bvs, i, row_peers[i])
        b.brk[pl.ds(y * NX, NX)] = b.bsk[pl.ds(y * NX, NX)]
        b.brv[pl.ds(x * NY, NY)] = b.bsv[pl.ds(x * NY, NY)]
        b.rim_out[0, 0] = b.wk[(QB + 1) * BLOCK :].astype(BF16)
        b.rim_out[0, 1] = b.wv[(QB + 1) * BLOCK :].astype(BF16)
        b.rim_out[1, 0] = b.wk[0:BLOCK].astype(BF16)
        b.rim_out[1, 1] = b.wv[0:BLOCK].astype(BF16)
        for i in range(4):
            send(b.rim_out.at[i // 2, i % 2], b.rim_in.at[i // 2, i % 2], sems[h].rim, i, after if i < 2 else before)

    def reduce_values(h):
        b = bufs[h]
        for i, d in enumerate(range(1, NX)):
            arrive(b.brv.at[pl.ds(lax.rem(x + NX - d, NX) * NY, NY)], sems[h].bvs, i)

        @pl.loop(0, NY)
        def _(row):
            sums = [jnp.zeros((BLOCK, HD), F32) for _ in range(QB)]
            for c in range(NX):
                term = b.brv[c * NY + row].astype(F32)
                local = jnp.full((BLOCK, HD), tv[c * NY + row], jnp.int32)
                for i in range(QB):
                    sums[i] = sums[i] + jnp.where(local == i, term, 0.0)
            for i in range(QB):
                b.av[row, i * BLOCK : (i + 1) * BLOCK] = sums[i]

        b.su[0, 0:half] = b.av[across, 0:half].astype(BF16)
        b.sd[0, half:TOK] = b.av[across, half:TOK].astype(BF16)
        send(b.su.at[0, 0:half], b.ru.at[0, 0:half], sems[h].bup, 0, up)
        send(b.sd.at[0, half:TOK], b.rd.at[0, half:TOK], sems[h].bdown, 0, down)

    def reduce_keys(h):
        b = bufs[h]
        for i, d in enumerate(range(1, NY)):
            arrive(b.brk.at[pl.ds(lax.rem(y + NY - d, NY) * NX, NX)], sems[h].bks, i)

        @pl.loop(0, NX)
        def _(col):
            sums = [jnp.zeros((BLOCK, HD), F32) for _ in range(QB)]
            for r in range(NY):
                term = b.brk[r * NX + col].astype(F32)
                local = jnp.full((BLOCK, HD), tk[r * NX + col], jnp.int32)
                for i in range(QB):
                    sums[i] = sums[i] + jnp.where(local == i, term, 0.0)
            for i in range(QB):
                b.ak[col, i * BLOCK : (i + 1) * BLOCK] = sums[i].astype(BF16)

        for i, d in enumerate(range(1, NX)):
            send(b.ak.at[lax.rem(x + d, NX)], b.rak.at[x], sems[h].axs, i, row_peers[i])
        b.rak[x] = b.ak[x]

    def ring_step(h, s):
        b = bufs[h]
        rows = slice(0, half) if s == 1 else slice(0, TOK)
        arrive(b.ru.at[s - 1, rows], sems[h].bup, s - 1)
        ahead = lax.rem(y + 4 - s, NY)
        b.su[s, rows] = (b.av[ahead, rows] + b.ru[s - 1, rows].astype(F32)).astype(BF16)
        if s == 1:
            b.su[s, half:TOK] = b.av[ahead, half:TOK].astype(BF16)
        send(b.su.at[s], b.ru.at[s], sems[h].bup, s, up)
        rows = slice(half, TOK) if s == 1 else slice(0, TOK)
        arrive(b.rd.at[s - 1, rows], sems[h].bdown, s - 1)
        behind = lax.rem(y + 4 + s, NY)
        b.sd[s, rows] = (b.av[behind, rows] + b.rd[s - 1, rows].astype(F32)).astype(BF16)
        if s == 1:
            b.sd[s, 0:half] = b.av[behind, 0:half].astype(BF16)
        send(b.sd.at[s], b.rd.at[s], sems[h].bdown, s, down)

    def finish(h):
        b = bufs[h]
        cols = slice(h * HD, (h + 1) * HD)
        for i in range(4):
            arrive(b.rim_in.at[i // 2, i % 2], sems[h].rim, i)
        for i, d in enumerate(range(1, NX)):
            arrive(b.rak.at[lax.rem(x + NX - d, NX)], sems[h].axs, i)
        keys = b.wk[BLOCK : BLOCK + TOK]
        for c in range(NX):
            keys = keys + b.rak[c].astype(F32)
        last = slice(TOK - BLOCK, TOK)
        kg_ref[:, cols] = keys.astype(BF16)
        kg_ref[0:BLOCK, cols] = (keys[0:BLOCK] + b.rim_in[0, 0].astype(F32)).astype(BF16)
        kg_ref[last, cols] = (keys[last] + b.rim_in[1, 0].astype(F32)).astype(BF16)
        arrive(b.ru.at[3], sems[h].bup, 3)
        arrive(b.rd.at[3], sems[h].bdown, 3)
        vals = b.wv[BLOCK : BLOCK + TOK] + b.av[y] + b.ru[3].astype(F32) + b.rd[3].astype(F32)
        vg_ref[:, cols] = vals.astype(BF16)
        vg_ref[0:BLOCK, cols] = (vals[0:BLOCK] + b.rim_in[0, 1].astype(F32)).astype(BF16)
        vg_ref[last, cols] = (vals[last] + b.rim_in[1, 1].astype(F32)).astype(BF16)

    for h, b in enumerate(bufs):
        for i, d in enumerate(range(1, NY)):
            arrive(b.rk.at[pl.ds(lax.rem(y + NY - d, NY) * NX, NX)], sems[h].ks, i)
        for i, d in enumerate(range(1, NX)):
            arrive(b.rv.at[pl.ds(lax.rem(x + NX - d, NX) * NY, NY)], sems[h].vs, i)
        compute(h)
        send_back(h)
    for h in range(KVH):
        reduce_values(h)
        reduce_keys(h)
        for s in range(1, 4):
            ring_step(h, s)
    for h in range(KVH):
        finish(h)
    for c in started:
        c.wait_send()


def local(queries, keys, values, out_grad, rand_blocks, global_blocks):
    vmem = pl.BlockSpec(memory_space=pltpu.VMEM)
    smem = pl.BlockSpec(memory_space=pltpu.SMEM)
    sems = []
    for _ in range(KVH):
        for _, n in HEAD_COPIES:
            sems += [pltpu.SemaphoreType.DMA((n,))] * 2
    return pl.pallas_call(
        kernel,
        out_shape=(
            jax.ShapeDtypeStruct(queries.shape, BF16),
            jax.ShapeDtypeStruct(queries.shape, BF16),
            jax.ShapeDtypeStruct(keys.shape, BF16),
            jax.ShapeDtypeStruct(keys.shape, BF16),
        ),
        in_specs=[smem, smem, vmem, vmem, vmem, vmem],
        out_specs=(vmem, vmem, vmem, vmem),
        scratch_shapes=[
            pltpu.SMEM((NY * NX,), jnp.int32),
            pltpu.SMEM((NX * NY,), jnp.int32),
            pltpu.SMEM((NY * NX,), jnp.int32),
            pltpu.VMEM((2, 2, BLOCK, KVH * HD), BF16),
            pltpu.VMEM((KEYS, HD), BF16),
            pltpu.VMEM((KEYS, HD), BF16),
            *[pltpu.VMEM(shape, dtype) for _ in range(KVH) for _, shape, dtype in HEAD_BUFFERS],
            pltpu.SemaphoreType.DMA((4,)),
            pltpu.SemaphoreType.DMA((4,)),
            *sems,
        ],
        compiler_params=pltpu.CompilerParams(collective_id=0, has_side_effects=True),
        name="genome_attention",
    )(rand_blocks, global_blocks, queries, keys, values, out_grad)


def solution(mesh):
    tokens, parts = P(("dp", "seq"), None), P("dp", None)
    return jax.shard_map(
        local,
        mesh=mesh,
        in_specs=(tokens, tokens, tokens, tokens, parts, P("dp")),
        out_specs=(tokens, tokens, tokens, tokens),
        check_vma=False,
    )
```

time: 229 us -> 120 us (0.52)
  the two profiles are of different devices: /device:TPU:698 before, /device:TPU:32 now
where the time goes in v1:
time: 120 us
  Pallas kernels  113 us (94%)
  local copies, waits for them, and re-layouts  5.97 us (5%)
    pallas_call x1, Pallas kernels, local(): pl.pallas_call(kernel, out_shape=(jax.ShapeDtypeStruct(queries.shape, BF1...  113 us
    unnamed x11, local copies, waits for them, and re-layouts  5.97 us

profile of v1, /device:TPU:32, one launch (start us, length us, event | category | flops | bytes accessed | tf_op | source)
XLA Modules:
  0.0 119.8 jit_solution(12452527670997715845)
XLA Ops:
  0.6 1.4 %copy.10.rb = s32[128,3]{1,0:T(8,128)} copy(s32[128,3]{0,1:T(4,128)} %param.10) | data formatting | bytes 3072 | tf_op args[4]
  2.0 113.2 %genome_attention.1 = (bf16[256,1024]{1,0:T(8,128)(2,1)}, bf16[256,1024]{1,0:T(8,128)(2,1)}, bf16[256,256]{1,0:T(8,128)(2,1)}, bf16[256,256]{1,0:T(8,128)(2,1)}) custom-call(s32[128,3]{1,0:T(8,128)} %copy.10.rb, s32[2]{0:T(128)} %gb.1, bf16[256,1024]{1,0:T(8,128)(2,1)} %q_ref.1, bf16[256,256]{1,0:T(8,128)(2,1)} %k_ref.1, bf16[256,256]{1,0:T(8,128)(2,1)} %v_ref.1, ...), custom_call_target="tpu_custom_call" | custom-call | tf_op jit(solution)/shard_map/genome_attention/pallas_call | solution.py:410
  115.3 0.0 copy-start
  115.3 1.9 %copy.15 = bf16[256,1024]{1,0:T(8,128)(2,1)} copy(bf16[256,1024]{1,0:T(8,128)(2,1)} %get-tuple-element.8) | data formatting | bytes 1048576
  117.2 0.0 copy-done
  117.2 0.0 copy-start.2
  117.2 0.8 copy.16
  118.0 0.2 copy-done.2
  118.2 0.0 copy-start.1
  118.2 0.7 copy.17
  118.9 0.3 copy-done.1
  119.2 0.7 copy.18
Async XLA Ops:
  115.3 1.9 %copy-start = (bf16[256,1024]{1,0:T(8,128)(2,1)S(1)}, bf16[256,1024]{1,0:T(8,128)(2,1)}, u32[]{:S(2)}) copy-start(bf16[256,1024]{1,0:T(8,128)(2,1)} %get-tuple-element.9) | copy-start | bytes 1572868
  117.2 1.0 copy-start.2
  118.2 1.0 copy-start.1

commit v2 on v1

--- a/solution.py
+++ b/solution.py
@@ -78,7 +78,7 @@
             setattr(self, name, ref)
 
 
-def kernel(rb, gb, q_ref, k_ref, v_ref, g_ref, out_ref, qg_ref, kg_ref, vg_ref, *scratch):
+def kernel(rb, gb, q_hbm, k_ref, v_ref, g_hbm, out_ref, qg_ref, kg_ref, vg_ref, *scratch):
     scratch = list(scratch)
 
     def take(n):
@@ -86,7 +86,7 @@
         del scratch[:n]
         return got
 
-    tk, tv, ent, halo, kc, vc = take(6)
+    tk, tv, ent, halo, kc, vc, q_ref, g_ref, load_sems = take(9)
     bufs = [Named([b[0] for b in HEAD_BUFFERS], take(len(HEAD_BUFFERS))) for _ in range(KVH)]
     halo_sems = take(2)
     sems = []
@@ -110,6 +110,9 @@
     for peer in peers:
         pl.semaphore_signal(barrier, inc=1, device_id={"seq": peer}, device_id_type=pl.DeviceIdType.MESH)
 
+    loads = [pltpu.make_async_copy(q_hbm, q_ref, load_sems.at[0]), pltpu.make_async_copy(g_hbm, g_ref, load_sems.at[1])]
+    for c in loads:
+        c.start()
     started = []
 
     def copy(src, dst, pair, i, peer):
@@ -149,7 +152,7 @@
     send(v_ref.at[0:BLOCK], halo.at[1, 1], halo_sems, 3, before)
 
     def listed(device):
-        ids = [rb[device * QB + e // RAND, e % RAND] for e in range(RAND * QB)]
+        ids = [rb[e % RAND, device * QB + e // RAND] for e in range(RAND * QB)]
         return ids + [gb[e] for e in range(GLOB)]
 
     def named(ids, owner, pick):
@@ -224,6 +227,9 @@
         b.kx[BLOCK + TOK :] = halo[1, 0, :, cols]
         b.vx[BLOCK + TOK :] = halo[1, 1, :, cols]
 
+    for c in loads:
+        c.wait()
+
     def compute(h):
         b = bufs[h]
         for ref in (b.wk, b.wv, b.gk, b.gv):
@@ -241,7 +247,7 @@
             kc[0:window] = b.kx[span]
             vc[0:window] = b.vx[span]
             for i in range(RAND):
-                owner = rb[me * QB + j, i] >> 2
+                owner = rb[i, me * QB + j] >> 2
                 to = slice(window + globe + i * BLOCK, window + globe + (i + 1) * BLOCK)
                 kc[to] = b.rk[owner]
                 vc[to] = b.rv[(owner & 3) * NY + (owner >> 2)]
@@ -389,33 +395,40 @@
             arrive(b.rv.at[pl.ds(lax.rem(x + NX - d, NX) * NY, NY)], sems[h].vs, i)
         compute(h)
         send_back(h)
-    for h in range(KVH):
-        reduce_values(h)
-        reduce_keys(h)
-        for s in range(1, 4):
+    reduce_values(0)
+    reduce_values(1)
+    for s in range(1, 4):
+        for h in range(KVH):
             ring_step(h, s)
+        if s <= KVH:
+            reduce_keys(s - 1)
     for h in range(KVH):
         finish(h)
     for c in started:
         c.wait_send()
 
 
+def store(*refs):
+    copies = [pltpu.make_async_copy(refs[i], refs[4 + i], refs[8].at[i]) for i in range(4)]
+    for c in copies:
+        c.start()
+    for c in copies:
+        c.wait()
+
+
 def local(queries, keys, values, out_grad, rand_blocks, global_blocks):
     vmem = pl.BlockSpec(memory_space=pltpu.VMEM)
     smem = pl.BlockSpec(memory_space=pltpu.SMEM)
+    hbm = pl.BlockSpec(memory_space=pl.ANY)
     sems = []
     for _ in range(KVH):
         for _, n in HEAD_COPIES:
             sems += [pltpu.SemaphoreType.DMA((n,))] * 2
-    return pl.pallas_call(
+    shapes = [queries.shape, queries.shape, keys.shape, keys.shape]
+    held = pl.pallas_call(
         kernel,
-        out_shape=(
-            jax.ShapeDtypeStruct(queries.shape, BF16),
-            jax.ShapeDtypeStruct(queries.shape, BF16),
-            jax.ShapeDtypeStruct(keys.shape, BF16),
-            jax.ShapeDtypeStruct(keys.shape, BF16),
-        ),
-        in_specs=[smem, smem, vmem, vmem, vmem, vmem],
+        out_shape=tuple(pltpu.VMEM(shape, BF16) for shape in shapes),
+        in_specs=[smem, smem, hbm, vmem, vmem, hbm],
         out_specs=(vmem, vmem, vmem, vmem),
         scratch_shapes=[
             pltpu.SMEM((NY * NX,), jnp.int32),
@@ -424,6 +437,9 @@
             pltpu.VMEM((2, 2, BLOCK, KVH * HD), BF16),
             pltpu.VMEM((KEYS, HD), BF16),
             pltpu.VMEM((KEYS, HD), BF16),
+            pltpu.VMEM(queries.shape, BF16),
+            pltpu.VMEM(queries.shape, BF16),
+            pltpu.SemaphoreType.DMA((2,)),
             *[pltpu.VMEM(shape, dtype) for _ in range(KVH) for _, shape, dtype in HEAD_BUFFERS],
             pltpu.SemaphoreType.DMA((4,)),
             pltpu.SemaphoreType.DMA((4,)),
@@ -431,7 +447,15 @@
         ],
         compiler_params=pltpu.CompilerParams(collective_id=0, has_side_effects=True),
         name="genome_attention",
-    )(rand_blocks, global_blocks, queries, keys, values, out_grad)
+    )(rand_blocks.T, global_blocks, queries, keys, values, out_grad)
+    return pl.pallas_call(
+        store,
+        out_shape=tuple(jax.ShapeDtypeStruct(shape, BF16) for shape in shapes),
+        in_specs=[vmem] * 4,
+        out_specs=(hbm,) * 4,
+        scratch_shapes=[pltpu.SemaphoreType.DMA((4,))],
+        name="store_outputs",
+    )(*[pltpu.with_memory_space_constraint(array, pltpu.VMEM) for array in held])
 
 
 def solution(mesh):

time: 120 us -> 108 us (0.900)
  the two profiles are of different devices: /device:TPU:32 before, /device:TPU:4 now
where the time goes in v2:
time: 108 us
  Pallas kernels  107 us (99%)
    pallas_call x1, Pallas kernels, local(): pl.pallas_call(kernel, out_shape=tuple((pltpu.VMEM(shape, BF16) for shape...  106 us

profile of v2, /device:TPU:4, one launch (start us, length us, event | category | flops | bytes accessed | tf_op | source)
XLA Modules:
  0.0 107.9 jit_solution(10256572113759069749)
XLA Ops:
  0.6 106.2 %genome_attention.1 = (bf16[256,1024]{1,0:T(8,128)(2,1)S(1)}, bf16[256,1024]{1,0:T(8,128)(2,1)S(1)}, bf16[256,256]{1,0:T(8,128)(2,1)S(1)}, bf16[256,256]{1,0:T(8,128)(2,1)S(1)}) custom-call(s32[3,128]{1,0:T(4,128)} %bitcast.1, s32[2]{0:T(128)} %gb.1, bf16[256,1024]{1,0:T(8,128)(2,1)} %q_hbm.1, bf16[256,256]{1,0:T(8,128)(2,1)} %k_ref.1, ...), custom_call_target="tpu_custom_call" | custom-call | tf_op jit(solution)/shard_map/genome_attention/pallas_call | solution.py:428
  106.8 1.1 %store_outputs.1 = (bf16[256,1024]{1,0:T(8,128)(2,1)}, bf16[256,1024]{1,0:T(8,128)(2,1)}, bf16[256,256]{1,0:T(8,128)(2,1)}, bf16[256,256]{1,0:T(8,128)(2,1)}) custom-call(bf16[256,1024]{1,0:T(8,128)(2,1)S(1)} %get-tuple-element.8.refs_0_, bf16[256,1024]{1,0:T(8,128)(2,1)S(1)} %get-tuple-element.9.refs_1_, bf16[256,256]{1,0:T(8,128)(2,1)S(1)} %get-tuple-element.10.refs_2_, ...), custom_call_target="tpu_custom_call" | custom-call | tf_op jit(solution)/shard_map/store_outputs/pallas_call | solution.py:451

commit v3 on v2

--- a/solution.py
+++ b/solution.py
@@ -16,6 +16,8 @@
 QB = 4
 NY = 8
 NX = 4
+NEAR = 5
+ROW_ORDER = (4, 3, 5, 2, 6, 1, 7)
 FAR = RAND * QB + GLOB
 KEYS = (3 + GLOB + RAND) * BLOCK
 TOK = QB * BLOCK
@@ -39,7 +41,8 @@
 
 HEAD_BUFFERS = (
     ("xg", (NX * QB, BLOCK, HD), BF16),
-    ("yg", (NY * QB, BLOCK, HD), BF16),
+    ("yn", (NEAR * QB, BLOCK, HD), BF16),
+    ("yf", ((NY - NEAR) * QB, BLOCK, HD), BF16),
     ("sk", (NY * NX, BLOCK, HD), BF16),
     ("rk", (NY * NX, BLOCK, HD), BF16),
     ("sv", (NX * NY, BLOCK, HD), BF16),
@@ -67,8 +70,8 @@
     ("rim_in", (2, 2, BLOCK, HD), BF16),
 )
 HEAD_COPIES = (
-    ("xs", NX - 1), ("up", 4), ("down", 4), ("ks", NY - 1), ("vs", NX - 1),
-    ("bks", NY - 1), ("bvs", NX - 1), ("axs", NX - 1), ("bup", 4), ("bdown", 4), ("rim", 4),
+    ("xs", NX - 1), ("up", 4), ("down", 4), ("ks", NY - 1), ("vn", NX - 1), ("vf", NX - 1),
+    ("bks", NY - 1), ("bvn", NX - 1), ("bvf", NX - 1), ("axs", NX - 1), ("bup", 4), ("bdown", 4), ("rim", 4),
 )
 
 
@@ -132,24 +135,34 @@
     for h, b in enumerate(bufs):
         cols = slice(h * HD, (h + 1) * HD)
         b.xg[pl.ds(x * QB, QB)] = k_ref[:, cols].reshape(QB, BLOCK, HD)
-        b.yg[pl.ds(y * QB, QB)] = v_ref[:, cols].reshape(QB, BLOCK, HD)
+        b.yn[2 * QB : 3 * QB] = v_ref[:, cols].reshape(QB, BLOCK, HD)
         b.kx[BLOCK : BLOCK + TOK] = k_ref[:, cols]
         b.vx[BLOCK : BLOCK + TOK] = v_ref[:, cols]
 
     pl.semaphore_wait(barrier, len(peers))
 
+    def held(b, i, first=0, n=QB):
+        ref, i = (b.yn, i) if i < NEAR else (b.yf, i - NEAR)
+        return ref.at[i * QB + first : i * QB + first + n]
+
+    def ring_out(h, s):
+        b = bufs[h]
+        n = QB if s < 3 else QB // 2
+        send(held(b, (2 - s) % NY, 0, n), held(b, (1 - s) % NY, 0, n), sems[h].up, s, up)
+        send(held(b, 2 + s, QB - n, n), held(b, 3 + s, QB - n, n), sems[h].down, s, down)
+
+    def ring_in(h, s):
+        b = bufs[h]
+        n = QB if s < 3 else QB // 2
+        arrive(held(b, (1 - s) % NY, 0, n), sems[h].up, s)
+        arrive(held(b, 3 + s, QB - n, n), sems[h].down, s)
+
+    for h in range(KVH):
+        ring_out(h, 0)
     for h, b in enumerate(bufs):
-        cols = slice(h * HD, (h + 1) * HD)
-        own = b.yg.at[pl.ds(y * QB, QB)]
-        send(own, own, sems[h].up, 0, up)
-        send(own, own, sems[h].down, 0, down)
         own = b.xg.at[pl.ds(x * QB, QB)]
         for i, peer in enumerate(row_peers):
             send(own, own, sems[h].xs, i, peer)
-    send(k_ref.at[TOK - BLOCK : TOK], halo.at[0, 0], halo_sems, 0, after)
-    send(v_ref.at[TOK - BLOCK : TOK], halo.at[0, 1], halo_sems, 1, after)
-    send(k_ref.at[0:BLOCK], halo.at[1, 0], halo_sems, 2, before)
-    send(v_ref.at[0:BLOCK], halo.at[1, 1], halo_sems, 3, before)
 
     def listed(device):
         ids = [rb[e % RAND, device * QB + e // RAND] for e in range(RAND * QB)]
@@ -170,8 +183,9 @@
     @pl.loop(0, NX)
     def _(col):
         ids = listed(y * NX + col)
-        for r in range(NY):
-            tv[col * NY + r] = named(ids, r * NX + x, lambda e, block: block & 3)
+        for i in range(NY):
+            owner = lax.rem(y + i + NY - 2, NY) * NX + x
+            tv[col * NY + i] = named(ids, owner, lambda e, block: block & 3)
 
     mine = listed(me)
 
@@ -180,19 +194,9 @@
         ent[owner] = jnp.maximum(named(mine, owner, lambda e, block: jnp.int32(e)), 0)
 
     half = TOK // 2
-    for s in range(1, 4):
-        for h, b in enumerate(bufs):
-            lower, upper = lax.rem(y + NY - s, NY) * QB, lax.rem(y + s, NY) * QB
-            n = QB if s < 3 else QB // 2
-            arrive(b.yg.at[pl.ds(lower, QB)], sems[h].up, s - 1)
-            part = b.yg.at[pl.ds(lower, n)]
-            send(part, part, sems[h].up, s, up)
-            arrive(b.yg.at[pl.ds(upper, QB)], sems[h].down, s - 1)
-            part = b.yg.at[pl.ds(upper + QB - n, n)]
-            send(part, part, sems[h].down, s, down)
-
-    across = lax.rem(y + 4, NY)
-    for h, b in enumerate(bufs):
+
+    def send_keys(h):
+        b = bufs[h]
         for i, d in enumerate(range(1, NX)):
             arrive(b.xg.at[pl.ds(lax.rem(x + NX - d, NX) * QB, QB)], sems[h].xs, i)
 
@@ -201,22 +205,48 @@
             for c in range(NX):
                 b.sk[row * NX + c] = b.xg[c * QB + jnp.maximum(tk[row * NX + c], 0)]
 
-        for i, d in enumerate(range(1, NY)):
+        for d in ROW_ORDER:
             row = lax.rem(y + d, NY)
-            send(b.sk.at[pl.ds(row * NX, NX)], b.rk.at[pl.ds(y * NX, NX)], sems[h].ks, i, col_peers[i])
+            send(b.sk.at[pl.ds(row * NX, NX)], b.rk.at[pl.ds(y * NX, NX)], sems[h].ks, d - 1, col_peers[d - 1])
         b.rk[pl.ds(y * NX, NX)] = b.sk[pl.ds(y * NX, NX)]
-        arrive(b.yg.at[pl.ds(across * QB, QB // 2)], sems[h].up, 3)
-        arrive(b.yg.at[pl.ds(across * QB + QB // 2, QB // 2)], sems[h].down, 3)
+
+    def send_values(h, near):
+        b = bufs[h]
+        first, n = (0, NEAR) if near else (NEAR, NY - NEAR)
+        ref = b.yn if near else b.yf
 
         @pl.loop(0, NX)
         def _(col):
-            for r in range(NY):
-                b.sv[col * NY + r] = b.yg[r * QB + jnp.maximum(tv[col * NY + r], 0)]
+            for i in range(n):
+                b.sv[col * NY + first + i] = ref[i * QB + jnp.maximum(tv[col * NY + first + i], 0)]
 
         for i, d in enumerate(range(1, NX)):
             col = lax.rem(x + d, NX)
-            send(b.sv.at[pl.ds(col * NY, NY)], b.rv.at[pl.ds(x * NY, NY)], sems[h].vs, i, row_peers[i])
-        b.rv[pl.ds(x * NY, NY)] = b.sv[pl.ds(x * NY, NY)]
+            send(
+                b.sv.at[pl.ds(col * NY + first, n)], b.rv.at[pl.ds(x * NY + first, n)],
+                sems[h].vn if near else sems[h].vf, i, row_peers[i],
+            )
+        b.rv[pl.ds(x * NY + first, n)] = b.sv[pl.ds(x * NY + first, n)]
+
+    for s in range(2):
+        for h in range(KVH):
+            ring_in(h, s)
+            ring_out(h, s + 1)
+    send_values(0, True)
+    send(k_ref.at[TOK - BLOCK : TOK], halo.at[0, 0], halo_sems, 0, after)
+    send(v_ref.at[TOK - BLOCK : TOK], halo.at[0, 1], halo_sems, 1, after)
+    send(k_ref.at[0:BLOCK], halo.at[1, 0], halo_sems, 2, before)
+    send(v_ref.at[0:BLOCK], halo.at[1, 1], halo_sems, 3, before)
+    for h in range(KVH):
+        ring_in(h, 2)
+        ring_out(h, 3)
+    send_keys(0)
+    ring_in(0, 3)
+    send_values(0, False)
+    send_values(1, True)
+    ring_in(1, 3)
+    send_values(1, False)
+    send_keys(1)
 
     for i in range(4):
         arrive(halo.at[i // 2, i % 2], halo_sems, i)
@@ -238,7 +268,7 @@
         for i in range(GLOB):
             owner = gb[i] >> 2
             kc[window + i * BLOCK : window + (i + 1) * BLOCK] = b.rk[owner]
-            vc[window + i * BLOCK : window + (i + 1) * BLOCK] = b.rv[(owner & 3) * NY + (owner >> 2)]
+            vc[window + i * BLOCK : window + (i + 1) * BLOCK] = b.rv[(owner & 3) * NY + (((owner >> 2) + NY + 2 - y) & 7)]
 
         @pl.loop(0, QB)
         def _(j):
@@ -250,7 +280,7 @@
                 owner = rb[i, me * QB + j] >> 2
                 to = slice(window + globe + i * BLOCK, window + globe + (i + 1) * BLOCK)
                 kc[to] = b.rk[owner]
-                vc[to] = b.rv[(owner & 3) * NY + (owner >> 2)]
+                vc[to] = b.rv[(owner & 3) * NY + (((owner >> 2) + NY + 2 - y) & 7)]
             base = h * GROUP * HD
             q = jnp.concatenate([q_ref[rows, base + i * HD : base + (i + 1) * HD] for i in range(GROUP)], axis=0)
             g = jnp.concatenate([g_ref[rows, base + i * HD : base + (i + 1) * HD] for i in range(GROUP)], axis=0)
@@ -281,27 +311,40 @@
         b.fk[RAND * QB :] = b.gk[...].astype(BF16).reshape(GLOB, BLOCK, HD)
         b.fv[RAND * QB :] = b.gv[...].astype(BF16).reshape(GLOB, BLOCK, HD)
 
-    def send_back(h):
-        b = bufs[h]
+    def pack_back(h):
+        b = bufs[h]
+
+        @pl.loop(0, NX)
+        def _(col):
+            for i in range(NY):
+                b.bsv[col * NY + i] = b.fv[ent[lax.rem(y + i + NY - 2, NY) * NX + col]]
 
         @pl.loop(0, NY * NX)
         def _(owner):
             b.bsk[owner] = b.fk[ent[owner]]
 
-        for i, d in enumerate(range(1, NY)):
+    def values_back(h):
+        b = bufs[h]
+        for near in (False, True):
+            first, n = (0, NEAR) if near else (NEAR, NY - NEAR)
+            for i, d in enumerate(range(1, NX)):
+                col = lax.rem(x + d, NX)
+                send(
+                    b.bsv.at[pl.ds(col * NY + first, n)], b.brv.at[pl.ds(x * NY + first, n)],
+                    sems[h].bvn if near else sems[h].bvf, i, row_peers[i],
+                )
+        b.brv[pl.ds(x * NY, NY)] = b.bsv[pl.ds(x * NY, NY)]
+
+    def keys_back(h, distances):
+        b = bufs[h]
+        for d in distances:
             row = lax.rem(y + d, NY)
-            send(b.bsk.at[pl.ds(row * NX, NX)], b.brk.at[pl.ds(y * NX, NX)], sems[h].bks, i, col_peers[i])
-
-        @pl.loop(0, NX)
-        def _(col):
-            for r in range(NY):
-                b.bsv[col * NY + r] = b.fv[ent[r * NX + col]]
-
-        for i, d in enumerate(range(1, NX)):
-            col = lax.rem(x + d, NX)
-            send(b.bsv.at[pl.ds(col * NY, NY)], b.brv.at[pl.ds(x * NY, NY)], sems[h].bvs, i, row_peers[i])
-        b.brk[pl.ds(y * NX, NX)] = b.bsk[pl.ds(y * NX, NX)]
-        b.brv[pl.ds(x * NY, NY)] = b.bsv[pl.ds(x * NY, NY)]
+            send(b.bsk.at[pl.ds(row * NX, NX)], b.brk.at[pl.ds(y * NX, NX)], sems[h].bks, d - 1, col_peers[d - 1])
+        if distances[-1] == ROW_ORDER[-1]:
+            b.brk[pl.ds(y * NX, NX)] = b.bsk[pl.ds(y * NX, NX)]
+
+    def rims_back(h):
+        b = bufs[h]
         b.rim_out[0, 0] = b.wk[(QB + 1) * BLOCK :].astype(BF16)
         b.rim_out[0, 1] = b.wv[(QB + 1) * BLOCK :].astype(BF16)
         b.rim_out[1, 0] = b.wk[0:BLOCK].astype(BF16)
@@ -309,12 +352,16 @@
         for i in range(4):
             send(b.rim_out.at[i // 2, i % 2], b.rim_in.at[i // 2, i % 2], sems[h].rim, i, after if i < 2 else before)
 
-    def reduce_values(h):
-        b = bufs[h]
+    def reduce_values(h, near):
+        b = bufs[h]
+        first, n = (0, NEAR) if near else (NEAR, NY - NEAR)
         for i, d in enumerate(range(1, NX)):
-            arrive(b.brv.at[pl.ds(lax.rem(x + NX - d, NX) * NY, NY)], sems[h].bvs, i)
-
-        @pl.loop(0, NY)
+            arrive(
+                b.brv.at[pl.ds(lax.rem(x + NX - d, NX) * NY + first, n)],
+                sems[h].bvn if near else sems[h].bvf, i,
+            )
+
+        @pl.loop(first, first + n)
         def _(row):
             sums = [jnp.zeros((BLOCK, HD), F32) for _ in range(QB)]
             for c in range(NX):
@@ -325,10 +372,11 @@
             for i in range(QB):
                 b.av[row, i * BLOCK : (i + 1) * BLOCK] = sums[i]
 
-        b.su[0, 0:half] = b.av[across, 0:half].astype(BF16)
-        b.sd[0, half:TOK] = b.av[across, half:TOK].astype(BF16)
-        send(b.su.at[0, 0:half], b.ru.at[0, 0:half], sems[h].bup, 0, up)
-        send(b.sd.at[0, half:TOK], b.rd.at[0, half:TOK], sems[h].bdown, 0, down)
+        if not near:
+            b.su[0, 0:half] = b.av[6, 0:half].astype(BF16)
+            b.sd[0, half:TOK] = b.av[6, half:TOK].astype(BF16)
+            send(b.su.at[0, 0:half], b.ru.at[0, 0:half], sems[h].bup, 0, up)
+            send(b.sd.at[0, half:TOK], b.rd.at[0, half:TOK], sems[h].bdown, 0, down)
 
     def reduce_keys(h):
         b = bufs[h]
@@ -354,14 +402,13 @@
         b = bufs[h]
         rows = slice(0, half) if s == 1 else slice(0, TOK)
         arrive(b.ru.at[s - 1, rows], sems[h].bup, s - 1)
-        ahead = lax.rem(y + 4 - s, NY)
+        ahead, behind = 6 - s, (6 + s) % NY
         b.su[s, rows] = (b.av[ahead, rows] + b.ru[s - 1, rows].astype(F32)).astype(BF16)
         if s == 1:
             b.su[s, half:TOK] = b.av[ahead, half:TOK].astype(BF16)
         send(b.su.at[s], b.ru.at[s], sems[h].bup, s, up)
         rows = slice(half, TOK) if s == 1 else slice(0, TOK)
         arrive(b.rd.at[s - 1, rows], sems[h].bdown, s - 1)
-        behind = lax.rem(y + 4 + s, NY)
         b.sd[s, rows] = (b.av[behind, rows] + b.rd[s - 1, rows].astype(F32)).astype(BF16)
         if s == 1:
             b.sd[s, 0:half] = b.av[behind, 0:half].astype(BF16)
@@ -383,7 +430,7 @@
         kg_ref[last, cols] = (keys[last] + b.rim_in[1, 0].astype(F32)).astype(BF16)
         arrive(b.ru.at[3], sems[h].bup, 3)
         arrive(b.rd.at[3], sems[h].bdown, 3)
-        vals = b.wv[BLOCK : BLOCK + TOK] + b.av[y] + b.ru[3].astype(F32) + b.rd[3].astype(F32)
+        vals = b.wv[BLOCK : BLOCK + TOK] + b.av[2] + b.ru[3].astype(F32) + b.rd[3].astype(F32)
         vg_ref[:, cols] = vals.astype(BF16)
         vg_ref[0:BLOCK, cols] = (vals[0:BLOCK] + b.rim_in[0, 1].astype(F32)).astype(BF16)
         vg_ref[last, cols] = (vals[last] + b.rim_in[1, 1].astype(F32)).astype(BF16)
@@ -392,16 +439,28 @@
         for i, d in enumerate(range(1, NY)):
             arrive(b.rk.at[pl.ds(lax.rem(y + NY - d, NY) * NX, NX)], sems[h].ks, i)
         for i, d in enumerate(range(1, NX)):
-            arrive(b.rv.at[pl.ds(lax.rem(x + NX - d, NX) * NY, NY)], sems[h].vs, i)
+            col = lax.rem(x + NX - d, NX) * NY
+            arrive(b.rv.at[pl.ds(col, NEAR)], sems[h].vn, i)
+            arrive(b.rv.at[pl.ds(col + NEAR, NY - NEAR)], sems[h].vf, i)
         compute(h)
-        send_back(h)
-    reduce_values(0)
-    reduce_values(1)
-    for s in range(1, 4):
-        for h in range(KVH):
-            ring_step(h, s)
-        if s <= KVH:
-            reduce_keys(s - 1)
+        pack_back(h)
+        values_back(h)
+        keys_back(h, ROW_ORDER if h == 0 else ROW_ORDER[:2])
+    keys_back(1, ROW_ORDER[2:])
+    for h in range(KVH):
+        rims_back(h)
+    reduce_values(0, False)
+    reduce_values(1, False)
+    reduce_values(0, True)
+    ring_step(0, 1)
+    ring_step(1, 1)
+    reduce_keys(0)
+    reduce_values(1, True)
+    ring_step(0, 2)
+    ring_step(1, 2)
+    reduce_keys(1)
+    ring_step(0, 3)
+    ring_step(1, 3)
     for h in range(KVH):
         finish(h)
     for c in started:

time: 108 us -> 101 us (0.935)
  the two profiles are of different devices: /device:TPU:4 before, /device:TPU:32 now
where the time goes in v3:
time: 101 us
  Pallas kernels  101 us (100%)
    pallas_call x1, Pallas kernels, local(): pl.pallas_call(kernel, out_shape=tuple((pltpu.VMEM(shape, BF16) for shape...  99.6 us

profile of v3, /device:TPU:32, one launch (start us, length us, event | category | flops | bytes accessed | tf_op | source)
XLA Modules:
  0.0 101.3 jit_solution(15663979341915934194)
XLA Ops:
  0.6 99.6 %genome_attention.1 = (bf16[256,1024]{1,0:T(8,128)(2,1)S(1)}, bf16[256,1024]{1,0:T(8,128)(2,1)S(1)}, bf16[256,256]{1,0:T(8,128)(2,1)S(1)}, bf16[256,256]{1,0:T(8,128)(2,1)S(1)}) custom-call(s32[3,128]{1,0:T(4,128)} %bitcast.1, s32[2]{0:T(128)} %gb.1, bf16[256,1024]{1,0:T(8,128)(2,1)} %q_hbm.1, bf16[256,256]{1,0:T(8,128)(2,1)} %k_ref.1, ...), custom_call_target="tpu_custom_call" | custom-call | tf_op jit(solution)/shard_map/genome_attention/pallas_call | solution.py:487
  100.2 1.1 %store_outputs.1 = (bf16[256,1024]{1,0:T(8,128)(2,1)}, bf16[256,1024]{1,0:T(8,128)(2,1)}, bf16[256,256]{1,0:T(8,128)(2,1)}, bf16[256,256]{1,0:T(8,128)(2,1)}) custom-call(bf16[256,1024]{1,0:T(8,128)(2,1)S(1)} %get-tuple-element.8.refs_0_, bf16[256,1024]{1,0:T(8,128)(2,1)S(1)} %get-tuple-element.9.refs_1_, bf16[256,256]{1,0:T(8,128)(2,1)S(1)} %get-tuple-element.10.refs_2_, ...), custom_call_target="tpu_custom_call" | custom-call | tf_op jit(solution)/shard_map/store_outputs/pallas_call | solution.py:510

commit v4 on v3

--- a/solution.py
+++ b/solution.py
@@ -157,6 +157,10 @@
         arrive(held(b, (1 - s) % NY, 0, n), sems[h].up, s)
         arrive(held(b, 3 + s, QB - n, n), sems[h].down, s)
 
+    send(k_ref.at[TOK - BLOCK : TOK], halo.at[0, 0], halo_sems, 0, after)
+    send(v_ref.at[TOK - BLOCK : TOK], halo.at[0, 1], halo_sems, 1, after)
+    send(k_ref.at[0:BLOCK], halo.at[1, 0], halo_sems, 2, before)
+    send(v_ref.at[0:BLOCK], halo.at[1, 1], halo_sems, 3, before)
     for h in range(KVH):
         ring_out(h, 0)
     for h, b in enumerate(bufs):
@@ -233,10 +237,6 @@
             ring_in(h, s)
             ring_out(h, s + 1)
     send_values(0, True)
-    send(k_ref.at[TOK - BLOCK : TOK], halo.at[0, 0], halo_sems, 0, after)
-    send(v_ref.at[TOK - BLOCK : TOK], halo.at[0, 1], halo_sems, 1, after)
-    send(k_ref.at[0:BLOCK], halo.at[1, 0], halo_sems, 2, before)
-    send(v_ref.at[0:BLOCK], halo.at[1, 1], halo_sems, 3, before)
     for h in range(KVH):
         ring_in(h, 2)
         ring_out(h, 3)

time: 101 us -> 100 us (0.990)
  the two profiles are of different devices: /device:TPU:32 before, /device:TPU:900 now
where the time goes in v4:
time: 100 us; the launch traced here: 99.9 us
  Pallas kernels  99.3 us (99%)
    pallas_call x1, Pallas kernels, local(): pl.pallas_call(kernel, out_shape=tuple((pltpu.VMEM(shape, BF16) for shape...  98.2 us

profile of v4, /device:TPU:900, one launch (start us, length us, event | category | flops | bytes accessed | tf_op | source)
XLA Modules:
  0.0 99.9 jit_solution(11875945989258109204)
XLA Ops:
  0.6 98.2 %genome_attention.1 = (bf16[256,1024]{1,0:T(8,128)(2,1)S(1)}, bf16[256,1024]{1,0:T(8,128)(2,1)S(1)}, bf16[256,256]{1,0:T(8,128)(2,1)S(1)}, bf16[256,256]{1,0:T(8,128)(2,1)S(1)}) custom-call(s32[3,128]{1,0:T(4,128)} %bitcast.1, s32[2]{0:T(128)} %gb.1, bf16[256,1024]{1,0:T(8,128)(2,1)} %q_hbm.1, bf16[256,256]{1,0:T(8,128)(2,1)} %k_ref.1, ...), custom_call_target="tpu_custom_call" | custom-call | tf_op jit(solution)/shard_map/genome_attention/pallas_call | solution.py:487
  98.9 1.1 %store_outputs.1 = (bf16[256,1024]{1,0:T(8,128)(2,1)}, bf16[256,1024]{1,0:T(8,128)(2,1)}, bf16[256,256]{1,0:T(8,128)(2,1)}, bf16[256,256]{1,0:T(8,128)(2,1)}) custom-call(bf16[256,1024]{1,0:T(8,128)(2,1)S(1)} %get-tuple-element.8.refs_0_, bf16[256,1024]{1,0:T(8,128)(2,1)S(1)} %get-tuple-element.9.refs_1_, bf16[256,256]{1,0:T(8,128)(2,1)S(1)} %get-tuple-element.10.refs_2_, ...), custom_call_target="tpu_custom_call" | custom-call | tf_op jit(solution)/shard_map/store_outputs/pallas_call | solution.py:510

commit v5 on v4

--- a/solution.py
+++ b/solution.py
@@ -311,7 +311,7 @@
         b.fk[RAND * QB :] = b.gk[...].astype(BF16).reshape(GLOB, BLOCK, HD)
         b.fv[RAND * QB :] = b.gv[...].astype(BF16).reshape(GLOB, BLOCK, HD)
 
-    def pack_back(h):
+    def pack_values_back(h):
         b = bufs[h]
 
         @pl.loop(0, NX)
@@ -319,9 +319,13 @@
             for i in range(NY):
                 b.bsv[col * NY + i] = b.fv[ent[lax.rem(y + i + NY - 2, NY) * NX + col]]
 
-        @pl.loop(0, NY * NX)
-        def _(owner):
-            b.bsk[owner] = b.fk[ent[owner]]
+    def pack_keys_back(h):
+        b = bufs[h]
+
+        @pl.loop(0, NY)
+        def _(row):
+            for c in range(NX):
+                b.bsk[row * NX + c] = b.fk[ent[row * NX + c]]
 
     def values_back(h):
         b = bufs[h]
@@ -443,8 +447,9 @@
             arrive(b.rv.at[pl.ds(col, NEAR)], sems[h].vn, i)
             arrive(b.rv.at[pl.ds(col + NEAR, NY - NEAR)], sems[h].vf, i)
         compute(h)
-        pack_back(h)
+        pack_values_back(h)
         values_back(h)
+        pack_keys_back(h)
         keys_back(h, ROW_ORDER if h == 0 else ROW_ORDER[:2])
     keys_back(1, ROW_ORDER[2:])
     for h in range(KVH):

time: 100 us -> 99.8 us (level)
  no operation moved by 1% of the time
where the time goes in v5:
time: 99.8 us; the launch traced here: 99.6 us
  Pallas kernels  99 us (99%)
    pallas_call x1, Pallas kernels, local(): pl.pallas_call(kernel, out_shape=tuple((pltpu.VMEM(shape, BF16) for shape...  97.9 us

profile of v5, /device:TPU:900, one launch (start us, length us, event | category | flops | bytes accessed | tf_op | source)
XLA Modules:
  0.0 99.6 jit_solution(11682521189881081971)
XLA Ops:
  0.6 97.9 %genome_attention.1 = (bf16[256,1024]{1,0:T(8,128)(2,1)S(1)}, bf16[256,1024]{1,0:T(8,128)(2,1)S(1)}, bf16[256,256]{1,0:T(8,128)(2,1)S(1)}, bf16[256,256]{1,0:T(8,128)(2,1)S(1)}) custom-call(s32[3,128]{1,0:T(4,128)} %bitcast.1, s32[2]{0:T(128)} %gb.1, bf16[256,1024]{1,0:T(8,128)(2,1)} %q_hbm.1, bf16[256,256]{1,0:T(8,128)(2,1)} %k_ref.1, ...), custom_call_target="tpu_custom_call" | custom-call | tf_op jit(solution)/shard_map/genome_attention/pallas_call | solution.py:492
  98.5 1.1 %store_outputs.1 = (bf16[256,1024]{1,0:T(8,128)(2,1)}, bf16[256,1024]{1,0:T(8,128)(2,1)}, bf16[256,256]{1,0:T(8,128)(2,1)}, bf16[256,256]{1,0:T(8,128)(2,1)}) custom-call(bf16[256,1024]{1,0:T(8,128)(2,1)S(1)} %get-tuple-element.8.refs_0_, bf16[256,1024]{1,0:T(8,128)(2,1)S(1)} %get-tuple-element.9.refs_1_, bf16[256,256]{1,0:T(8,128)(2,1)S(1)} %get-tuple-element.10.refs_2_, ...), custom_call_target="tpu_custom_call" | custom-call | tf_op jit(solution)/shard_map/store_outputs/pallas_call | solution.py:515
